TPU v7x, 128 devices: a whole 4x4x4 slice. The times are simulated.
128 devices in a mesh: row: 16 (over x_hi, y, core), col: 8 (over z, x_lo).
Axes of the slice: x: 4 (x_hi: 2, x_lo: 2; x = x_hi * 2 + x_lo), y: 4, z: 4, core: 2. Of those that a mesh axis runs over, the one named last changes fastest.
Arguments:
- values: float32 [8192, 8192], P('row', 'col'), may hold values from 0 to 10, as said below
- pattern: int32 [64, 64], replicated, may hold values from 0 to 1, as said below
- pruning: int32 [64, 64], replicated, may hold values from 0 to 1, as said below
- owners: int32 [64], replicated, may hold values from 0 to 63, as said below
Outputs:
- expanded: float32 [8192, 8192], P('row', 'col')
Inputs may be any that keep to these rules, and one draw needn't show every extreme that they name: `values`: positive scores. `pattern`: every diagonal block is present. `pruning`: every diagonal block is kept. `owners`: A permutation of the 64 column blocks. Of the 8 column blocks of one index of col, at most 2 are stored at the column blocks of any one index of col, and exactly 2 at those of some index.
All inputs are finite; a program needn't handle non-finite values.
Results may differ from a plain program's by a relative error of at most 0.00065.
Values may be sent and summed in bfloat16 or wider, within the bound.
No kernel may reach another device: no remote copies, remote signals or barrier semaphores. Data moves between devices by JAX's collectives and lax.ppermute only.
A program may use at most 128 MiB of HBM per device.

v0:
```python
import jax
import jax.numpy as jnp
from jax import lax
from jax.sharding import PartitionSpec as P

BLK = 128


def expand_mask(tile, mask, blk):
    rows_in, cols_in = tile.shape
    shaped = tile.reshape(rows_in // blk, blk, cols_in // blk, blk)
    return (shaped * mask.astype(tile.dtype)[:, None, :, None]).reshape(rows_in, cols_in)


def ranks_of(destination):
    width = destination.shape[-1]
    earlier = jnp.arange(width)[:, None] < jnp.arange(width)[None, :]
    same_dest = destination[..., :, None] == destination[..., None, :]
    return jnp.sum(jnp.where(same_dest & earlier, 1, 0), axis=-2).astype(jnp.int32)


def pack_blocks(tile, owners, me_col, ncols, capacity, blk):
    rows_in, cols_in = tile.shape
    width = cols_in // blk
    my_owners = lax.dynamic_slice(owners, (me_col * width,), (width,))
    destination = my_owners // width
    rank = ranks_of(destination)
    slot_ids = jnp.arange(ncols * capacity)
    selector = (
        (destination[None, :] == (slot_ids // capacity)[:, None])
        & (rank[None, :] == (slot_ids % capacity)[:, None])
    ).astype(tile.dtype)
    column_blocks = tile.reshape(rows_in, width, blk)
    outgoing = jnp.einsum(
        "pk,rkb->prb",
        selector,
        column_blocks,
        preferred_element_type=jnp.float32,
        precision=lax.Precision.HIGHEST,
    )
    return outgoing


def unpack_blocks(arrived, owners, me_col, ncols, capacity):
    slot_count, rows_in, blk = arrived.shape
    width = owners.shape[0] // ncols
    table = owners.reshape(ncols, width)
    rank = ranks_of(table // width)
    wanted = me_col * width + jnp.arange(width)
    matches = table[None, :, :] == wanted[:, None, None]
    which_slot = rank[:, :, None] == jnp.arange(capacity)[None, None, :]
    selector = jnp.sum(jnp.where(matches[:, :, :, None] & which_slot[None], 1, 0), axis=2)
    selector = selector.reshape(width, ncols * capacity).astype(arrived.dtype)
    placed = jnp.einsum(
        "sp,prb->rsb",
        selector,
        arrived,
        preferred_element_type=jnp.float32,
        precision=lax.Precision.HIGHEST,
    )
    return placed.reshape(rows_in, width * blk)


def body(values, pattern, pruning, owners):
    rows_dev, cols_dev = values.shape
    blk = BLK
    row_blocks = rows_dev // blk
    col_blocks = cols_dev // blk
    ncols = lax.axis_size("col")
    capacity = max(2, (col_blocks + ncols - 1) // ncols)
    me_row = lax.axis_index("row")
    me_col = lax.axis_index("col")
    local_pattern = lax.dynamic_slice(
        pattern, (me_row * row_blocks, me_col * col_blocks), (row_blocks, col_blocks)
    )
    masked = expand_mask(values, local_pattern, blk)
    colsum_in = lax.psum(jnp.sum(masked, axis=0), "row")
    stochastic = (masked / colsum_in[None, :]).astype(jnp.bfloat16)
    row_panel = lax.all_gather(stochastic, "col", axis=1, tiled=True)
    nodes = row_panel.shape[1]
    pruning_rows = lax.dynamic_slice(
        pruning, (me_row * row_blocks, 0), (row_blocks, pruning.shape[1])
    )
    kept_mask = lax.dynamic_slice_in_dim(pruning_rows, me_col * col_blocks, col_blocks, 1)
    square = jnp.dot(
        row_panel,
        lax.all_gather(stochastic, "row", axis=0, tiled=True),
        preferred_element_type=jnp.float32,
    )
    inflated = expand_mask(square * square, kept_mask, blk)
    colsum_out = lax.psum(jnp.sum(inflated, axis=0), "row")
    normalized = jnp.float32(nodes) * inflated / colsum_out[None, :]
    arrived_out = lax.all_to_all(
        pack_blocks(normalized, owners, me_col, ncols, capacity, blk),
        "col",
        split_axis=0,
        concat_axis=0,
        tiled=True,
    )
    result = unpack_blocks(arrived_out, owners, me_col, ncols, capacity)
    return result


def solution(mesh):
    return jax.shard_map(
        body,
        mesh=mesh,
        in_specs=(P("row", "col"), P(), P(), P()),
        out_specs=P("row", "col"),
        check_vma=False,
    )
```

profile of v0, /device:TPU:0, one launch (start us, length us, event | category | flops | bytes accessed | tf_op | source)
XLA Modules:
  0.0 452.6 jit_solution(7957865634004855820)
XLA Ops:
  6.5 0.0 all-gather.3.cloned.1.call-start
  6.5 0.9 dynamic-slice_convert_fusion.1
  7.4 0.2 mul.43
  7.7 0.5 copy-done
  8.1 0.7 fusion.2
  8.8 38.2 %psum.14 = f32[1024]{0:T(1024)S(1)} all-reduce(f32[1024]{0:T(1024)S(1)} %fusion.2), channel_id=1, replica_groups=mesh['row'=16,'col'=8] {'row'}, use_global_device_ids=true, to_apply=%region_2.0 | all-reduce | flops 1024 | bytes 8192 | tf_op jit(solution)/shard_map/psum | solution.py:77
  47.0 3.2 divide_convert_fusion
  50.2 0.0 all-gather.3.cloned.1.call-update
  50.3 0.0 all-gather.5.cloned.1.call-start
  50.3 0.7 all-gather.5.cloned.1.call-update
  51.0 0.0 copy-done.1
  51.0 0.1 and_select_fusion.2
  51.1 0.8 dynamic-slice_convert_fusion
  51.9 0.1 select_reduce_fusion.2
  52.0 164.6 %all-gather.3.cloned.1.call-done = bf16[512,8192]{1,0:T(8,128)(2,1)} async-done(((bf16[512,1024]{1,0:T(8,128)(2,1)}), bf16[512,8192]{1,0:T(8,128)(2,1)}) %all-gather.3.cloned.1.call-update) | async-done | bytes 8388624 | tf_op jit(solution)/shard_map/all_gather | solution.py:79
  216.6 112.1 %all-gather.5.cloned.1.call-done = bf16[8192,1024]{1,0:T(8,128)(2,1)} async-done(((bf16[512,1024]{1,0:T(8,128)(2,1)}), bf16[8192,1024]{1,0:T(8,128)(2,1)}) %all-gather.5.cloned.1.call-update) | async-done | bytes 16777232 | tf_op jit(solution)/shard_map/all_gather | solution.py:87
  328.7 0.2 mul.47
  328.9 14.8 %fusion.14 = (f32[1024]{0:T(1024)S(1)}, f32[512,1024]{1,0:T(8,128)S(1)}) fusion(f32[64,8,8,128]{3,2,1,0:T(8,128)S(1)} %bitcast.34, bf16[512,8192]{1,0:T(8,128)(2,1)} %all-gather.3.cloned.1.call-done, bf16[8192,1024]{1,0:T(8,128)(2,1)} %all-gather.5.cloned.1.call-done), kind=kOutput, calls=%fused_computation.43 | convolution fusion | flops 8591506432 | bytes 29364224 | tf_op jit(solution)/shard_map/dot_general | solution.py:85
  343.7 33.8 %psum.15 = f32[1024]{0:T(1024)S(1)} all-reduce(f32[1024]{0:T(1024)S(1)} %get-tuple-element.5), channel_id=1, replica_groups=mesh['row'=16,'col'=8] {'row'}, use_global_device_ids=true, to_apply=%region_4.5 | all-reduce | flops 1024 | bytes 8192 | tf_op jit(solution)/shard_map/psum | solution.py:91
  377.6 0.3 divide_bitcast_fusion
  377.8 0.5 copy.21
  378.3 1.9 fusion.5
  380.2 3.3 copy.12
  383.5 5.3 %all-to-all-start = ((f32[16,512,128]{2,1,0:T(8,128)}), f32[16,512,128]{2,1,0:T(8,128)}, u32[]{:S(2)}, u32[]{:S(2)}) async-start(f32[16,512,128]{2,1,0:T(8,128)} %copy.12), calls=%async_computation | async-start | bytes 8388608 | tf_op jit(solution)/shard_map/all_to_all | solution.py:93
  388.8 0.1 eq.99
  388.9 0.1 select_reduce_fusion.1
  389.0 0.1 broadcast_compare_fusion
  389.1 0.4 select_reduce_fusion
  389.5 0.1 copy.14
  389.6 47.6 %all-to-all-done = f32[16,512,128]{2,1,0:T(8,128)} async-done(((f32[16,512,128]{2,1,0:T(8,128)}), f32[16,512,128]{2,1,0:T(8,128)}, u32[]{:S(2)}, u32[]{:S(2)}) %all-to-all-start) | async-done | bytes 4194336 | tf_op jit(solution)/shard_map/all_to_all | solution.py:93
  437.1 6.8 %fusion = f32[512,128,8]{1,2,0:T(8,128)S(1)} fusion(f32[8,16,1]{0,1,2:T(8,128)S(1)} %bitcast.35, f32[16,512,128]{2,1,0:T(8,128)} %all-to-all-done), kind=kOutput, calls=%fused_computation | convolution fusion | flops 100663296 | bytes 6291968 | tf_op jit(solution)/shard_map/sp,prb->rsb/dot_general | solution.py:54
  444.0 1.8 copy.33
  (8 shorter events, 0.0 us)
Async XLA Ops:
  6.5 210.1 %all-gather.3.cloned.1.call-start = ((), (), s32[]{:S(2)}) async-start(), calls=%async_computation.1 | async-start | bytes 9437184 | tf_op jit(solution)/shard_map/all_gather | solution.py:79
  6.5 1.6 copy-start
  50.2 0.8 copy-start.1
  50.3 278.4 %all-gather.5.cloned.1.call-start = ((), (), s32[]{:S(2)}) async-start(), calls=%async_computation.2 | async-start | bytes 17825792 | tf_op jit(solution)/shard_map/all_gather | solution.py:87
  383.5 53.7 %all-to-all-start = ((f32[16,512,128]{2,1,0:T(8,128)}), f32[16,512,128]{2,1,0:T(8,128)}, u32[]{:S(2)}, u32[]{:S(2)}) async-start(f32[16,512,128]{2,1,0:T(8,128)} %copy.12), calls=%async_computation | async-start | bytes 8388608 | tf_op jit(solution)/shard_map/all_to_all | solution.py:93
Sparse Core Ops, SparseCore 0:
  50.4 166.1 all-gather.2
  219.0 109.6 all-gather.4
where the time goes:
time: 453 us
  waiting for transfers between devices  325 us (72%)
  blocking collectives  72 us (16%)
  matrix products  23.5 us (5%)
  between operations  13.5 us (3%)
  other arithmetic  6.6 us (1%)
  local copies, waits for them, and re-layouts  6.55 us (1%)
  starting transfers between devices  5.38 us (1%)
    all_gather x1, waiting for transfers between devices, body(): row_panel = lax.all_gather(stochastic, 'col', axis=1, tiled=True)  165 us
    all_gather x1, waiting for transfers between devices, body(): lax.all_gather(stochastic, 'row', axis=0, tiled=True)  112 us
    all_to_all x1, waiting for transfers between devices, body(): lax.all_to_all(pack_blocks(normalized, owners, me_col, ncols, capacity, b...  47.6 us
    psum x1, blocking collectives, body(): colsum_in = lax.psum(jnp.sum(masked, axis=0), 'row')  38.2 us
    psum x1, blocking collectives, body(): colsum_out = lax.psum(jnp.sum(inflated, axis=0), 'row')  33.8 us
    dot_general x1, matrix products, body(): jnp.dot(row_panel, lax.all_gather(stochastic, 'row', axis=0, tiled=True),...  14.8 us
  transfers between devices with their start and end apart: 3, of which 3 were waited for; matrix products, arithmetic and copies ran while one was open for 0% of the time, Pallas kernels for 0%

commit v1 on v0

--- a/solution.py
+++ b/solution.py
@@ -76,7 +76,8 @@
     masked = expand_mask(values, local_pattern, blk)
     colsum_in = lax.psum(jnp.sum(masked, axis=0), "row")
     stochastic = (masked / colsum_in[None, :]).astype(jnp.bfloat16)
-    row_panel = lax.all_gather(stochastic, "col", axis=1, tiled=True)
+    blocks = lax.all_gather(stochastic, "col", axis=0, tiled=False)
+    row_panel = jnp.concatenate(blocks, axis=1)
     nodes = row_panel.shape[1]
     pruning_rows = lax.dynamic_slice(
         pruning, (me_row * row_blocks, 0), (row_blocks, pruning.shape[1])

time: 453 us -> 453 us (level)
  local copies, waits for them, and re-layouts: 6.55 us -> 18 us
  waiting for transfers between devices: 325 us -> 314 us
    all_gather x1, waiting for transfers between devices: 112 us -> 101 us  [body(): lax.all_gather(stochastic, 'row', axis=0, tiled=True)]
    reshape x0 -> x1, local copies, waits for them, and re-layouts: none -> 11.4 us  [body(): row_panel = jnp.concatenate(blocks, axis=1)]
  transfers between devices with their start and end apart: 3 -> 3, of which waited for: 3 -> 3; matrix products, arithmetic and copies ran while one was open for 0% -> 3% of each run, Pallas kernels for 0% -> 0%
where the time goes in v1:
time: 453 us
  waiting for transfers between devices  314 us (69%)
  blocking collectives  72 us (16%)
  matrix products  23.6 us (5%)
  local copies, waits for them, and re-layouts  18 us (4%)
  between operations  13.5 us (3%)
  other arithmetic  6.6 us (1%)
  starting transfers between devices  5.38 us (1%)
    all_gather x1, waiting for transfers between devices, body(): blocks = lax.all_gather(stochastic, 'col', axis=0, tiled=False)  165 us
    all_gather x1, waiting for transfers between devices, body(): lax.all_gather(stochastic, 'row', axis=0, tiled=True)  101 us
    all_to_all x1, waiting for transfers between devices, body(): lax.all_to_all(pack_blocks(normalized, owners, me_col, ncols, capacity, b...  47.6 us
    psum x1, blocking collectives, body(): colsum_in = lax.psum(jnp.sum(masked, axis=0), 'row')  38.2 us
    psum x1, blocking collectives, body(): colsum_out = lax.psum(jnp.sum(inflated, axis=0), 'row')  33.8 us
    dot_general x1, matrix products, body(): jnp.dot(row_panel, lax.all_gather(stochastic, 'row', axis=0, tiled=True),...  14.9 us
    reshape x1, local copies, waits for them, and re-layouts, body(): row_panel = jnp.concatenate(blocks, axis=1)  11.4 us
  transfers between devices with their start and end apart: 3, of which 3 were waited for; matrix products, arithmetic and copies ran while one was open for 3% of the time, Pallas kernels for 0%

profile of v1, /device:TPU:0, one launch (start us, length us, event | category | flops | bytes accessed | tf_op | source)
XLA Modules:
  0.0 452.7 jit_solution(555574985806275335)
XLA Ops:
  6.5 0.0 all-gather.6.cloned.1.call-start
  6.5 0.9 dynamic-slice_convert_fusion.1
  7.4 0.2 mul.43
  7.7 0.5 copy-done
  8.1 0.7 fusion.2
  8.8 38.2 %psum.14 = f32[1024]{0:T(1024)S(1)} all-reduce(f32[1024]{0:T(1024)S(1)} %fusion.2), channel_id=1, replica_groups=mesh['row'=16,'col'=8] {'row'}, use_global_device_ids=true, to_apply=%region_2.0 | all-reduce | flops 1024 | bytes 8192 | tf_op jit(solution)/shard_map/psum | solution.py:77
  47.0 3.2 divide_convert_fusion
  50.2 0.0 all-gather.6.cloned.1.call-update
  50.3 0.0 all-gather.4.cloned.1.call-start
  50.3 0.7 all-gather.4.cloned.1.call-update
  51.0 0.1 and_select_fusion.2
  51.1 0.8 dynamic-slice_convert_fusion
  51.9 0.1 select_reduce_fusion.2
  52.0 164.6 %all-gather.6.cloned.1.call-done = bf16[4096,1024]{1,0:T(8,128)(2,1)} async-done(((bf16[512,1024]{1,0:T(8,128)(2,1)}), bf16[4096,1024]{1,0:T(8,128)(2,1)}) %all-gather.6.cloned.1.call-update) | async-done | bytes 8388624 | tf_op jit(solution)/shard_map/all_gather | solution.py:79
  216.6 11.4 %copy.18 = bf16[512,8,1024]{0,2,1:T(8,128)(2,1)} copy(bf16[512,8,1024]{2,0,1:T(8,128)(2,1)} %bitcast.36) | data formatting | bytes 16777216 | tf_op jit(solution)/shard_map/reshape | solution.py:80
  228.0 100.7 %all-gather.4.cloned.1.call-done = bf16[8192,1024]{1,0:T(8,128)(2,1)} async-done(((bf16[512,1024]{1,0:T(8,128)(2,1)}), bf16[8192,1024]{1,0:T(8,128)(2,1)}) %all-gather.4.cloned.1.call-update) | async-done | bytes 16777232 | tf_op jit(solution)/shard_map/all_gather | solution.py:88
  328.7 0.2 mul.47
  328.9 14.9 %fusion.14 = (f32[1024]{0:T(1024)S(1)}, f32[512,1024]{1,0:T(8,128)S(1)}) fusion(f32[64,8,8,128]{3,2,1,0:T(8,128)S(1)} %bitcast.40, bf16[512,8192]{0,1:T(8,128)(2,1)} %bitcast.37, bf16[8192,1024]{1,0:T(8,128)(2,1)} %all-gather.4.cloned.1.call-done), kind=kOutput, calls=%fused_computation.43 | convolution fusion | flops 8591506432 | bytes 29364224 | tf_op jit(solution)/shard_map/dot_general | solution.py:86
  343.8 33.8 %psum.15 = f32[1024]{0:T(1024)S(1)} all-reduce(f32[1024]{0:T(1024)S(1)} %get-tuple-element.5), channel_id=1, replica_groups=mesh['row'=16,'col'=8] {'row'}, use_global_device_ids=true, to_apply=%region_4.5 | all-reduce | flops 1024 | bytes 8192 | tf_op jit(solution)/shard_map/psum | solution.py:92
  377.6 0.3 divide_bitcast_fusion
  377.9 0.5 copy.28
  378.4 1.9 fusion.5
  380.3 3.3 copy.19
  383.6 5.3 %all-to-all-start = ((f32[16,512,128]{2,1,0:T(8,128)}), f32[16,512,128]{2,1,0:T(8,128)}, u32[]{:S(2)}, u32[]{:S(2)}) async-start(f32[16,512,128]{2,1,0:T(8,128)} %copy.19), calls=%async_computation | async-start | bytes 8388608 | tf_op jit(solution)/shard_map/all_to_all | solution.py:94
  388.9 0.1 eq.99
  389.0 0.1 select_reduce_fusion.1
  389.1 0.1 broadcast_compare_fusion
  389.2 0.4 select_reduce_fusion
  389.6 0.1 copy.21
  389.6 47.6 %all-to-all-done = f32[16,512,128]{2,1,0:T(8,128)} async-done(((f32[16,512,128]{2,1,0:T(8,128)}), f32[16,512,128]{2,1,0:T(8,128)}, u32[]{:S(2)}, u32[]{:S(2)}) %all-to-all-start) | async-done | bytes 4194336 | tf_op jit(solution)/shard_map/all_to_all | solution.py:94
  437.2 6.8 %fusion = f32[512,128,8]{1,2,0:T(8,128)S(1)} fusion(f32[8,16,1]{0,1,2:T(8,128)S(1)} %bitcast.41, f32[16,512,128]{2,1,0:T(8,128)} %all-to-all-done), kind=kOutput, calls=%fused_computation | convolution fusion | flops 100663296 | bytes 6291968 | tf_op jit(solution)/shard_map/sp,prb->rsb/dot_general | solution.py:54
  444.1 1.8 copy.40
  (9 shorter events, 0.0 us)
Async XLA Ops:
  6.5 210.0 %all-gather.6.cloned.1.call-start = ((), (), s32[]{:S(2)}) async-start(), calls=%async_computation.2 | async-start | bytes 9437184 | tf_op jit(solution)/shard_map/all_gather | solution.py:79
  6.5 1.6 copy-start
  50.2 0.8 copy-start.1
  50.3 278.4 %all-gather.4.cloned.1.call-start = ((), (), s32[]{:S(2)}) async-start(), calls=%async_computation.1 | async-start | bytes 17825792 | tf_op jit(solution)/shard_map/all_gather | solution.py:88
  383.6 53.7 %all-to-all-start = ((f32[16,512,128]{2,1,0:T(8,128)}), f32[16,512,128]{2,1,0:T(8,128)}, u32[]{:S(2)}, u32[]{:S(2)}) async-start(f32[16,512,128]{2,1,0:T(8,128)} %copy.19), calls=%async_computation | async-start | bytes 8388608 | tf_op jit(solution)/shard_map/all_to_all | solution.py:94
Sparse Core Ops, SparseCore 0:
  50.4 166.1 all-gather.5
  219.0 109.6 all-gather.3

commit v2 on v0

--- a/solution.py
+++ b/solution.py
@@ -4,6 +4,11 @@
 from jax.sharding import PartitionSpec as P
 
 BLK = 128
+
+
+def exchange_gather(value, mesh_axis, dim):
+    stack = jnp.stack([value] * lax.axis_size(mesh_axis))
+    return jnp.concatenate(lax.all_to_all(stack, mesh_axis, 0, 0), axis=dim)
 
 
 def expand_mask(tile, mask, blk):
@@ -83,9 +88,7 @@
     )
     kept_mask = lax.dynamic_slice_in_dim(pruning_rows, me_col * col_blocks, col_blocks, 1)
     square = jnp.dot(
-        row_panel,
-        lax.all_gather(stochastic, "row", axis=0, tiled=True),
-        preferred_element_type=jnp.float32,
+        row_panel, exchange_gather(stochastic, "row", 0), preferred_element_type=jnp.float32
     )
     inflated = expand_mask(square * square, kept_mask, blk)
     colsum_out = lax.psum(jnp.sum(inflated, axis=0), "row")

time: 453 us -> 536 us (1.18)
  waiting for transfers between devices: 325 us -> 389 us
  blocking collectives: 72 us -> 78.9 us
  starting transfers between devices: 5.38 us -> 11.7 us
  local copies, waits for them, and re-layouts: 6.55 us -> 12.7 us
    all_gather x1, waiting for transfers between devices: 165 us -> 329 us  [body(): row_panel = lax.all_gather(stochastic, 'col', axis=1, tiled=True)]
    all_gather x1 -> x0, waiting for transfers between devices: 112 us -> none  [body(): lax.all_gather(stochastic, 'row', axis=0, tiled=True)]
    all_to_all x0 -> x1, waiting for transfers between devices: none -> 15.8 us  [exchange_gather(): return jnp.concatenate(lax.all_to_all(stack, mesh_axis, 0, 0), axis=dim)]
    psum x1, blocking collectives: 33.8 us -> 40.7 us  [body(): colsum_out = lax.psum(jnp.sum(inflated, axis=0), 'row')]
    another operation x0 -> x1, local copies, waits for them, and re-layouts: none -> 6.17 us  [exchange_gather(): stack = jnp.stack([value] * lax.axis_size(mesh_axis))]
where the time goes in v2:
time: 536 us; the launch traced here: 535 us
  waiting for transfers between devices  389 us (73%)
  blocking collectives  78.9 us (15%)
  matrix products  23.5 us (4%)
  between operations  13.5 us (3%)
  local copies, waits for them, and re-layouts  12.7 us (2%)
  starting transfers between devices  11.7 us (2%)
  other arithmetic  5.63 us (1%)
    all_gather x1, waiting for transfers between devices, body(): row_panel = lax.all_gather(stochastic, 'col', axis=1, tiled=True)  329 us
    all_to_all x1, waiting for transfers between devices, body(): lax.all_to_all(pack_blocks(normalized, owners, me_col, ncols, capacity, b...  43.8 us
    psum x1, blocking collectives, body(): colsum_out = lax.psum(jnp.sum(inflated, axis=0), 'row')  40.7 us
    psum x1, blocking collectives, body(): colsum_in = lax.psum(jnp.sum(masked, axis=0), 'row')  38.2 us
    all_to_all x1, waiting for transfers between devices, exchange_gather(): return jnp.concatenate(lax.all_to_all(stack, mesh_axis, 0, 0), axis=dim)  15.8 us
    dot_general x1, matrix products, body(): jnp.dot(row_panel, exchange_gather(stochastic, 'row', 0), preferred_eleme...  14.8 us
  transfers between devices with their start and end apart: 3, of which 3 were waited for; matrix products, arithmetic and copies ran while one was open for 0% of the time, Pallas kernels for 0%

profile of v2, /device:TPU:0, one launch (start us, length us, event | category | flops | bytes accessed | tf_op | source)
XLA Modules:
  0.0 535.2 jit_solution(4094026461271154416)
XLA Ops:
  6.5 0.9 dynamic-slice_convert_fusion.1
  7.4 0.2 mul.43
  7.7 0.5 copy-done.1
  8.1 0.7 fusion.2
  8.8 38.2 %psum.14 = f32[1024]{0:T(1024)S(1)} all-reduce(f32[1024]{0:T(1024)S(1)} %fusion.2), channel_id=1, replica_groups=mesh['row'=16,'col'=8] {'row'}, use_global_device_ids=true, to_apply=%region_2.0 | all-reduce | flops 1024 | bytes 8192 | tf_op jit(solution)/shard_map/psum | solution.py:82
  47.0 2.2 divide_convert_fusion
  49.3 0.0 copy-start
  49.3 6.2 %stack.2 = bf16[16,512,1024]{2,1,0:T(8,128)(2,1)} broadcast(bf16[512,1024]{1,0:T(8,128)(2,1)S(1)} %divide_convert_fusion), dimensions={1,2} | broadcast | bytes 17825792 | tf_op jit(solution)/shard_map/stack | solution.py:10
  55.5 5.3 all-to-all-start
  60.8 0.0 all-gather.2.cloned.1.call-start
  60.8 0.7 all-gather.2.cloned.1.call-update
  61.5 0.1 and_select_fusion.2
  61.6 0.8 dynamic-slice_convert_fusion
  62.4 0.1 select_reduce_fusion.2
  62.5 328.9 %all-gather.2.cloned.1.call-done = bf16[512,8192]{1,0:T(8,128)(2,1)} async-done(((bf16[512,1024]{1,0:T(8,128)(2,1)}), bf16[512,8192]{1,0:T(8,128)(2,1)}) %all-gather.2.cloned.1.call-update) | async-done | bytes 8388624 | tf_op jit(solution)/shard_map/all_gather | solution.py:84
  391.4 15.8 %all-to-all-done = bf16[16,512,1024]{2,1,0:T(8,128)(2,1)} async-done(((bf16[16,512,1024]{2,1,0:T(8,128)(2,1)}), bf16[16,512,1024]{2,1,0:T(8,128)(2,1)}, u32[]{:S(2)}, u32[]{:S(2)}) %all-to-all-start) | async-done | bytes 16777248 | tf_op jit(solution)/shard_map/all_to_all | solution.py:11
  407.2 0.2 mul.47
  407.4 14.8 %fusion.14 = (f32[1024]{0:T(1024)S(1)}, f32[512,1024]{1,0:T(8,128)S(1)}) fusion(f32[64,8,8,128]{3,2,1,0:T(8,128)S(1)} %bitcast.35, bf16[512,8192]{1,0:T(8,128)(2,1)} %all-gather.2.cloned.1.call-done, bf16[8192,1024]{1,0:T(8,128)(2,1)} %bitcast.1), kind=kOutput, calls=%fused_computation.43 | convolution fusion | flops 8591506432 | bytes 29364224 | tf_op jit(solution)/shard_map/dot_general | solution.py:90
  422.2 40.7 %psum.15 = f32[1024]{0:T(1024)S(1)} all-reduce(f32[1024]{0:T(1024)S(1)} %get-tuple-element.5), channel_id=1, replica_groups=mesh['row'=16,'col'=8] {'row'}, use_global_device_ids=true, to_apply=%region_4.5 | all-reduce | flops 1024 | bytes 8192 | tf_op jit(solution)/shard_map/psum | solution.py:94
  462.9 0.3 divide_bitcast_fusion
  463.2 0.5 copy.21
  463.7 1.9 fusion.5
  465.6 3.3 copy.12
  468.8 6.3 %all-to-all-start.1 = ((f32[16,512,128]{2,1,0:T(8,128)}), f32[16,512,128]{2,1,0:T(8,128)}, u32[]{:S(2)}, u32[]{:S(2)}) async-start(f32[16,512,128]{2,1,0:T(8,128)} %copy.12), calls=%async_computation.1 | async-start | bytes 8388608 | tf_op jit(solution)/shard_map/all_to_all | solution.py:96
  475.2 0.1 eq.99
  475.3 0.1 select_reduce_fusion.1
  475.4 0.1 broadcast_compare_fusion
  475.4 0.4 select_reduce_fusion
  475.8 0.1 copy.14
  475.9 43.8 %all-to-all-done.1 = f32[16,512,128]{2,1,0:T(8,128)} async-done(((f32[16,512,128]{2,1,0:T(8,128)}), f32[16,512,128]{2,1,0:T(8,128)}, u32[]{:S(2)}, u32[]{:S(2)}) %all-to-all-start.1) | async-done | bytes 4194336 | tf_op jit(solution)/shard_map/all_to_all | solution.py:96
  519.7 6.8 %fusion = f32[512,128,8]{1,2,0:T(8,128)S(1)} fusion(f32[8,16,1]{0,1,2:T(8,128)S(1)} %bitcast.36, f32[16,512,128]{2,1,0:T(8,128)} %all-to-all-done.1), kind=kOutput, calls=%fused_computation | convolution fusion | flops 100663296 | bytes 6291968 | tf_op jit(solution)/shard_map/sp,prb->rsb/dot_general | solution.py:59
  526.6 1.8 copy.33
  (10 shorter events, 0.0 us)
Async XLA Ops:
  6.5 1.6 copy-start.1
  49.3 6.2 %copy-start = (bf16[512,1024]{1,0:T(8,128)(2,1)}, bf16[512,1024]{1,0:T(8,128)(2,1)S(1)}, u32[]{:S(2)}) copy-start(bf16[512,1024]{1,0:T(8,128)(2,1)S(1)} %divide_convert_fusion) | copy-start | bytes 3145732
  55.5 6.0 %copy-start.2 = (s32[64]{0:T(128)S(1)}, s32[64]{0:T(128)}, u32[]{:S(2)}) copy-start(s32[64]{0:T(128)} %param.7) | copy-start | bytes 772
  55.5 351.8 %all-to-all-start = ((bf16[16,512,1024]{2,1,0:T(8,128)(2,1)}), bf16[16,512,1024]{2,1,0:T(8,128)(2,1)}, u32[]{:S(2)}, u32[]{:S(2)}) async-start(bf16[16,512,1024]{2,1,0:T(8,128)(2,1)} %stack.2), calls=%async_computation | async-start | bytes 33554432 | tf_op jit(solution)/shard_map/all_to_all | solution.py:11
  60.8 330.6 %all-gather.2.cloned.1.call-start = ((), (), s32[]{:S(2)}) async-start(), calls=%async_computation.2 | async-start | bytes 9437184 | tf_op jit(solution)/shard_map/all_gather | solution.py:84
  468.8 50.9 %all-to-all-start.1 = ((f32[16,512,128]{2,1,0:T(8,128)}), f32[16,512,128]{2,1,0:T(8,128)}, u32[]{:S(2)}, u32[]{:S(2)}) async-start(f32[16,512,128]{2,1,0:T(8,128)} %copy.12), calls=%async_computation.1 | async-start | bytes 8388608 | tf_op jit(solution)/shard_map/all_to_all | solution.py:96
Sparse Core Ops, SparseCore 0:
  63.2 328.1 all-gather.1
